TPU v7x, 256 devices: a whole 4x4x8 slice. The times are simulated.
256 devices in a mesh: row: 16 (over x_hi, y, core), col: 16 (over z, x_lo).
Axes of the slice: x: 4 (x_hi: 2, x_lo: 2; x = x_hi * 2 + x_lo), y: 4, z: 8, core: 2. Of those that a mesh axis runs over, the one named last changes fastest.
Arguments:
- inputs: bfloat16 [2048, 4096], P('row', 'col'), may hold values from -6 to 6
- grad_output: bfloat16 [2048, 4096], P('row', 'col'), may hold values from -6 to 6
- gate_pre: bfloat16 [2048, 14336], P('col', 'row'), may hold values from -6 to 6
- up_pre: bfloat16 [2048, 14336], P('col', 'row'), may hold values from -6 to 6
- gate_weight: bfloat16 [14336, 4096], P('row', 'col'), may hold values from -0.09375 to 0.09375
- up_weight: bfloat16 [14336, 4096], P('row', 'col'), may hold values from -0.09375 to 0.09375
- down_weight: bfloat16 [14336, 4096], P('row', 'col'), may hold values from -0.046875 to 0.046875
Outputs:
- grad_input: float32 [2048, 4096], P('row', 'col')
- grad_gate_weight: float32 [14336, 4096], P('row', 'col')
- grad_up_weight: float32 [14336, 4096], P('row', 'col')
- grad_down_weight: float32 [14336, 4096], P('row', 'col')
All inputs are finite; a program needn't handle non-finite values.
Results may differ from a plain program's by a relative error of at most 0.0029.
Values may be sent and summed in bfloat16 or wider, within the bound.
No kernel may reach another device: no remote copies, remote signals or barrier semaphores. Data moves between devices by JAX's collectives and lax.ppermute only.
A program may use at most 64 MiB of HBM per device.

v0:
```python
import math
import jax
import jax.numpy as jnp
from jax import lax
from jax.sharding import PartitionSpec as P


def outer_sum(left_rows, right_rows):
    return lax.dot_general(
        left_rows, right_rows, (((0,), (0,)), ((), ())), preferred_element_type=jnp.float32
    )


def inner_last(left_rows, right_rows):
    return lax.dot_general(
        left_rows, right_rows, (((1,), (1,)), ((), ())), preferred_element_type=jnp.float32
    )


def shards(inputs, grad_output, gate_pre, up_pre, gate_weight, up_weight, down_weight):
    input_cols, output_cols = (
        lax.all_gather(inputs, "row", axis=0, tiled=True),
        lax.all_gather(grad_output, "row", axis=0, tiled=True),
    )
    gate_value = gate_pre.astype(jnp.float32)
    up_value = up_pre.astype(jnp.float32)
    sigmoid_gate = jax.nn.sigmoid(gate_value)
    silu_gate = gate_value * sigmoid_gate
    hidden = (silu_gate * up_value).astype(jnp.bfloat16)
    output_rows = output_cols
    grad_hidden = lax.psum_scatter(
        inner_last(output_rows, down_weight), "col", scatter_dimension=0, tiled=True
    )
    grad_gate_pre = (
        grad_hidden * up_value * sigmoid_gate * (1.0 + gate_value * (1.0 - sigmoid_gate))
    ).astype(jnp.bfloat16)
    grad_up_pre = (grad_hidden * silu_gate).astype(jnp.bfloat16)
    gate_piece = lax.all_gather(grad_gate_pre, "col", axis=0, tiled=True)
    up_piece = lax.all_gather(grad_up_pre, "col", axis=0, tiled=True)
    gate_running = outer_sum(gate_piece, input_cols)
    up_running = outer_sum(up_piece, input_cols)
    input_part = jnp.dot(gate_piece, gate_weight, preferred_element_type=jnp.float32) + jnp.dot(
        up_piece, up_weight, preferred_element_type=jnp.float32
    )
    partial_input = input_part
    first_three = (gate_running, up_running, partial_input)
    output_rows = output_cols
    grad_gate, grad_up, partial_input, grad_down = first_three + (
        outer_sum(lax.all_gather(hidden, "col", axis=0, tiled=True), output_rows),
    )
    grad_input = lax.psum_scatter(partial_input, "row", scatter_dimension=0, tiled=True)
    factor = 1.0 / math.sqrt(input_cols.shape[0])
    return (grad_input, grad_gate * factor, grad_up * factor, grad_down * factor)


def solution(mesh):
    placed = (
        P("row", "col"),
        P("row", "col"),
        P("col", "row"),
        P("col", "row"),
        P("row", "col"),
        P("row", "col"),
        P("row", "col"),
    )
    return jax.shard_map(
        shards,
        mesh=mesh,
        in_specs=placed,
        out_specs=(P("row", "col"), P("row", "col"), P("row", "col"), P("row", "col")),
        check_vma=False,
    )
```

profile of v0, /device:TPU:8, one launch (start us, length us, event | category | flops | bytes accessed | tf_op | source)
XLA Modules:
  0.0 645.6 jit_solution(3945084945116645436)
XLA Ops:
  7.2 0.0 copy-start
  7.2 0.0 all-gather.6.cloned.1.call-start
  7.2 0.7 all-gather.6.cloned.1.call-update
  7.9 0.0 reduce-scatter.3.cloned.1.call-start
  8.0 55.2 %all-gather.6.cloned.1.call-done = bf16[2048,256]{1,0:T(8,128)(2,1)} async-done(((bf16[128,256]{1,0:T(8,128)(2,1)}), bf16[2048,256]{1,0:T(8,128)(2,1)}) %all-gather.6.cloned.1.call-update) | async-done | bytes 1048592 | tf_op jit(solution)/shard_map/all_gather | solution.py:23
  63.2 0.0 copy-done
  63.2 5.5 fusion.8
  68.6 0.0 copy-start.5
  68.6 0.0 copy-start.6
  68.6 0.0 copy-start.4
  68.6 0.0 reduce-scatter.3.cloned.1.call-update
  68.7 0.0 all-gather.8.cloned.1.call-start
  68.7 161.0 %reduce-scatter.3.cloned.1.call-done = f32[128,896]{1,0:T(8,128)} async-done(((f32[2048,896]{1,0:T(8,128)}), f32[128,896]{1,0:T(8,128)}) %reduce-scatter.3.cloned.1.call-update) | async-done | bytes 458768 | tf_op jit(solution)/shard_map/reduce_scatter | solution.py:31
  229.7 0.0 copy-done.5
  229.7 0.0 copy-done.6
  229.7 2.1 multiply_convert_fusion
  231.8 0.0 all-gather.8.cloned.1.call-update
  231.8 0.0 all-gather.10.cloned.1.call-start
  231.8 0.5 all-gather.10.cloned.1.call-update
  232.4 0.0 all-gather.12.cloned.1.call-start
  232.4 0.5 all-gather.12.cloned.1.call-update
  233.0 0.0 all-gather.14.cloned.1.call-start
  233.0 0.5 all-gather.14.cloned.1.call-update
  233.5 0.0 copy-start.3
  233.5 0.0 reduce-scatter.5.cloned.1.call-start
  233.6 89.1 %all-gather.8.cloned.1.call-done = bf16[2048,896]{1,0:T(8,128)(2,1)} async-done(((bf16[128,896]{1,0:T(8,128)(2,1)}), bf16[2048,896]{1,0:T(8,128)(2,1)}) %all-gather.8.cloned.1.call-update) | async-done | bytes 3670032 | tf_op jit(solution)/shard_map/all_gather | solution.py:38
  322.7 0.0 copy-done.4
  322.7 3.3 fusion.9
  326.0 88.2 %all-gather.10.cloned.1.call-done = bf16[2048,896]{1,0:T(8,128)(2,1)} async-done(((bf16[128,896]{1,0:T(8,128)(2,1)}), bf16[2048,896]{1,0:T(8,128)(2,1)}) %all-gather.10.cloned.1.call-update) | async-done | bytes 3670032 | tf_op jit(solution)/shard_map/all_gather | solution.py:39
  414.2 0.0 copy-done.3
  414.2 4.7 convolution_add_fusion
  418.9 0.0 reduce-scatter.5.cloned.1.call-update
  418.9 46.7 %all-gather.12.cloned.1.call-done = bf16[2048,256]{1,0:T(8,128)(2,1)} async-done(((bf16[128,256]{1,0:T(8,128)(2,1)}), bf16[2048,256]{1,0:T(8,128)(2,1)}) %all-gather.12.cloned.1.call-update) | async-done | bytes 1048592 | tf_op jit(solution)/shard_map/all_gather | solution.py:22
  465.6 0.0 copy-start.1
  465.6 0.0 copy-start.7
  465.6 4.6 convolution_multiply_fusion.1
  470.2 0.0 copy-done.1
  470.2 0.0 copy-done.7
  470.2 0.0 copy-start.2
  470.2 2.1 convolution_multiply_fusion.2
  472.3 84.0 %all-gather.14.cloned.1.call-done = bf16[2048,896]{1,0:T(8,128)(2,1)} async-done(((bf16[128,896]{1,0:T(8,128)(2,1)}), bf16[2048,896]{1,0:T(8,128)(2,1)}) %all-gather.14.cloned.1.call-update) | async-done | bytes 3670032 | tf_op jit(solution)/shard_map/all_gather | solution.py:49
  556.3 0.0 copy-done.2
  556.3 4.1 convolution_multiply_fusion
  560.4 78.3 %reduce-scatter.5.cloned.1.call-done = f32[128,256]{1,0:T(8,128)} async-done(((f32[2048,256]{1,0:T(8,128)}), f32[128,256]{1,0:T(8,128)}) %reduce-scatter.5.cloned.1.call-update) | async-done | bytes 131088 | tf_op jit(solution)/shard_map/reduce_scatter | solution.py:51
Async XLA Ops:
  7.2 56.0 %copy-start = (bf16[896,256]{1,0:T(8,128)(2,1)S(1)}, bf16[896,256]{1,0:T(8,128)(2,1)}, u32[]{:S(2)}) copy-start(bf16[896,256]{1,0:T(8,128)(2,1)} %param.13) | copy-start | bytes 1376260
  7.2 56.0 %all-gather.6.cloned.1.call-start = ((), (), s32[]{:S(2)}) async-start(), calls=%async_computation.2 | async-start | bytes 1114112 | tf_op jit(solution)/shard_map/all_gather | solution.py:23
  7.9 221.8 %reduce-scatter.3.cloned.1.call-start = ((), (), s32[]{:S(2)}) async-start(), calls=%async_computation.3 | async-start | bytes 7798784 | tf_op jit(solution)/shard_map/reduce_scatter | solution.py:31
  68.6 161.0 %copy-start.5 = (bf16[128,896]{1,0:T(8,128)(2,1)S(1)}, bf16[128,896]{1,0:T(8,128)(2,1)}, u32[]{:S(2)}) copy-start(bf16[128,896]{1,0:T(8,128)(2,1)} %param.9) | copy-start | bytes 688132
  68.6 161.0 %copy-start.6 = (bf16[128,896]{1,0:T(8,128)(2,1)S(1)}, bf16[128,896]{1,0:T(8,128)(2,1)}, u32[]{:S(2)}) copy-start(bf16[128,896]{1,0:T(8,128)(2,1)} %param.10) | copy-start | bytes 688132
  68.6 254.1 %copy-start.4 = (bf16[896,256]{1,0:T(8,128)(2,1)S(1)}, bf16[896,256]{1,0:T(8,128)(2,1)}, u32[]{:S(2)}) copy-start(bf16[896,256]{1,0:T(8,128)(2,1)} %param.11) | copy-start | bytes 1376260
  68.7 254.0 %all-gather.8.cloned.1.call-start = ((), (), s32[]{:S(2)}) async-start(), calls=%async_computation.4 | async-start | bytes 3899392 | tf_op jit(solution)/shard_map/all_gather | solution.py:38
  231.8 182.4 %all-gather.10.cloned.1.call-start = ((), (), s32[]{:S(2)}) async-start(), calls=%async_computation.5 | async-start | bytes 3899392 | tf_op jit(solution)/shard_map/all_gather | solution.py:39
  232.4 233.3 %all-gather.12.cloned.1.call-start = ((), (), s32[]{:S(2)}) async-start(), calls=%async_computation.7 | async-start | bytes 1114112 | tf_op jit(solution)/shard_map/all_gather | solution.py:22
  233.0 323.4 %all-gather.14.cloned.1.call-start = ((), (), s32[]{:S(2)}) async-start(), calls=%async_computation.8 | async-start | bytes 3899392 | tf_op jit(solution)/shard_map/all_gather | solution.py:49
  233.5 180.6 %copy-start.3 = (bf16[896,256]{1,0:T(8,128)(2,1)S(1)}, bf16[896,256]{1,0:T(8,128)(2,1)}, u32[]{:S(2)}) copy-start(bf16[896,256]{1,0:T(8,128)(2,1)} %param.12) | copy-start | bytes 1376260
  233.5 405.2 %reduce-scatter.5.cloned.1.call-start = ((), (), s32[]{:S(2)}) async-start(), calls=%async_computation.6 | async-start | bytes 2228224 | tf_op jit(solution)/shard_map/reduce_scatter | solution.py:51
  465.6 4.6 copy-start.1
  465.6 4.6 copy-start.7
  470.2 86.1 %copy-start.2 = (bf16[2048,256]{1,0:T(8,128)(2,1)S(1)}, bf16[2048,256]{1,0:T(8,128)(2,1)}, u32[]{:S(2)}) copy-start(bf16[2048,256]{1,0:T(8,128)(2,1)} %all-gather.6.cloned.1.call-done) | copy-start | bytes 3145732
Sparse Core Ops, SparseCore 0:
  10.8 52.3 all-gather.5
  68.8 160.8 reduce-scatter.2
  232.0 90.5 all-gather.7
  324.9 89.2 all-gather.9
  416.8 48.8 all-gather.11
  467.3 88.9 all-gather.13
  561.1 77.6 reduce-scatter.4
where the time goes:
time: 646 us
  waiting for transfers between devices  605 us (94%)
  matrix products  24.2 us (4%)
  between operations  14.2 us (2%)
    reduce_scatter x1, waiting for transfers between devices, shards(): lax.psum_scatter(inner_last(output_rows, down_weight), 'col', scatter_dim...  161 us
    all_gather x1, waiting for transfers between devices, shards(): gate_piece = lax.all_gather(grad_gate_pre, 'col', axis=0, tiled=True)  89.1 us
    all_gather x1, waiting for transfers between devices, shards(): up_piece = lax.all_gather(grad_up_pre, 'col', axis=0, tiled=True)  88.2 us
    all_gather x1, waiting for transfers between devices, shards(): lax.all_gather(hidden, 'col', axis=0, tiled=True)  84 us
    reduce_scatter x1, waiting for transfers between devices, shards(): lax.psum_scatter(partial_input, 'row', scatter_dimension=0, tiled=True)  78.3 us
    all_gather x1, waiting for transfers between devices, shards(): lax.all_gather(grad_output, 'row', axis=0, tiled=True)  55.2 us
    all_gather x1, waiting for transfers between devices, shards(): lax.all_gather(inputs, 'row', axis=0, tiled=True)  46.7 us
  transfers between devices with their start and end apart: 7, of which 7 were waited for; matrix products, arithmetic and copies ran while one was open for 3% of the time, Pallas kernels for 0%

commit v1 on v0

--- a/solution.py
+++ b/solution.py
@@ -36,7 +36,9 @@
     ).astype(jnp.bfloat16)
     grad_up_pre = (grad_hidden * silu_gate).astype(jnp.bfloat16)
     gate_piece = lax.all_gather(grad_gate_pre, "col", axis=0, tiled=True)
-    up_piece = lax.all_gather(grad_up_pre, "col", axis=0, tiled=True)
+    up_piece = jnp.concatenate(
+        lax.all_to_all(jnp.stack([grad_up_pre] * lax.axis_size("col")), "col", 0, 0), axis=0
+    )
     gate_running = outer_sum(gate_piece, input_cols)
     up_running = outer_sum(up_piece, input_cols)
     input_part = jnp.dot(gate_piece, gate_weight, preferred_element_type=jnp.float32) + jnp.dot(

time: 646 us -> 617 us (0.955)
  waiting for transfers between devices: 605 us -> 566 us
  starting transfers between devices: 0.27 us -> 7.48 us
    all_gather x1 -> x0, waiting for transfers between devices: 88.2 us -> none  [shards(): up_piece = lax.all_gather(grad_up_pre, 'col', axis=0, tiled=True)]
    all_gather x1, waiting for transfers between devices: 89.1 us -> 141 us  [shards(): gate_piece = lax.all_gather(grad_gate_pre, 'col', axis=0, tiled=True)]
    all_to_all x0 -> x1, starting transfers between devices: none -> 7.24 us  [shards(): lax.all_to_all(jnp.stack([grad_up_pre] * lax.axis_size('col')), 'col', 0, 0)]
  transfers between devices with their start and end apart: 7 -> 7, of which waited for: 7 -> 6; matrix products, arithmetic and copies ran while one was open for 3% -> 3% of each run, Pallas kernels for 0% -> 0%
where the time goes in v1:
time: 617 us; the launch traced here: 616 us
  waiting for transfers between devices  566 us (92%)
  matrix products  24.2 us (4%)
  between operations  14.2 us (2%)
  starting transfers between devices  7.48 us (1%)
    reduce_scatter x1, waiting for transfers between devices, shards(): lax.psum_scatter(inner_last(output_rows, down_weight), 'col', scatter_dim...  161 us
    all_gather x1, waiting for transfers between devices, shards(): gate_piece = lax.all_gather(grad_gate_pre, 'col', axis=0, tiled=True)  141 us
    all_gather x1, waiting for transfers between devices, shards(): lax.all_gather(hidden, 'col', axis=0, tiled=True)  84 us
    reduce_scatter x1, waiting for transfers between devices, shards(): lax.psum_scatter(partial_input, 'row', scatter_dimension=0, tiled=True)  78.2 us
    all_gather x1, waiting for transfers between devices, shards(): lax.all_gather(grad_output, 'row', axis=0, tiled=True)  55.2 us
    all_gather x1, waiting for transfers between devices, shards(): lax.all_gather(inputs, 'row', axis=0, tiled=True)  44.5 us
  transfers between devices with their start and end apart: 7, of which 6 were waited for; matrix products, arithmetic and copies ran while one was open for 3% of the time, Pallas kernels for 0%

profile of v1, /device:TPU:8, one launch (start us, length us, event | category | flops | bytes accessed | tf_op | source)
XLA Modules:
  0.0 616.5 jit_solution(11039970918786801526)
XLA Ops:
  7.2 0.0 copy-start
  7.2 0.0 all-gather.5.cloned.1.call-start
  7.2 0.7 all-gather.5.cloned.1.call-update
  7.9 0.0 reduce-scatter.3.cloned.1.call-start
  8.0 55.2 %all-gather.5.cloned.1.call-done = bf16[2048,256]{1,0:T(8,128)(2,1)} async-done(((bf16[128,256]{1,0:T(8,128)(2,1)}), bf16[2048,256]{1,0:T(8,128)(2,1)}) %all-gather.5.cloned.1.call-update) | async-done | bytes 1048592 | tf_op jit(solution)/shard_map/all_gather | solution.py:23
  63.2 0.0 copy-done
  63.2 5.5 fusion.8
  68.6 0.0 copy-start.5
  68.6 0.0 copy-start.6
  68.6 0.0 reduce-scatter.3.cloned.1.call-update
  68.7 0.0 all-gather.7.cloned.1.call-start
  68.7 161.0 %reduce-scatter.3.cloned.1.call-done = f32[128,896]{1,0:T(8,128)} async-done(((f32[2048,896]{1,0:T(8,128)}), f32[128,896]{1,0:T(8,128)}) %reduce-scatter.3.cloned.1.call-update) | async-done | bytes 458768 | tf_op jit(solution)/shard_map/reduce_scatter | solution.py:31
  229.7 0.0 copy-done.5
  229.7 0.0 copy-done.6
  229.7 2.1 multiply_convert_fusion
  231.7 0.0 all-gather.7.cloned.1.call-update
  231.8 0.0 all-gather.9.cloned.1.call-start
  231.8 0.5 all-gather.9.cloned.1.call-update
  232.3 2.4 stack.2
  234.8 0.0 copy-start.4
  234.8 7.2 %all-to-all-start = ((bf16[16,128,896]{2,1,0:T(8,128)(2,1)}), bf16[16,128,896]{2,1,0:T(8,128)(2,1)}, u32[]{:S(2)}, u32[]{:S(2)}) async-start(bf16[16,128,896]{2,1,0:T(8,128)(2,1)} %stack.2), calls=%async_computation.1 | async-start | bytes 7340032 | tf_op jit(solution)/shard_map/all_to_all | solution.py:40
  242.0 0.0 all-gather.11.cloned.1.call-start
  242.1 0.5 all-gather.11.cloned.1.call-update
  242.6 0.0 copy-start.3
  242.6 0.0 reduce-scatter.5.cloned.1.call-start
  242.7 141.5 %all-gather.7.cloned.1.call-done = bf16[2048,896]{1,0:T(8,128)(2,1)} async-done(((bf16[128,896]{1,0:T(8,128)(2,1)}), bf16[2048,896]{1,0:T(8,128)(2,1)}) %all-gather.7.cloned.1.call-update) | async-done | bytes 3670032 | tf_op jit(solution)/shard_map/all_gather | solution.py:38
  384.1 0.0 copy-done.4
  384.1 3.3 fusion.9
  387.4 0.0 all-to-all-done
  387.4 0.0 copy-done.3
  387.5 4.7 convolution_add_fusion
  392.2 0.0 reduce-scatter.5.cloned.1.call-update
  392.2 44.5 %all-gather.9.cloned.1.call-done = bf16[2048,256]{1,0:T(8,128)(2,1)} async-done(((bf16[128,256]{1,0:T(8,128)(2,1)}), bf16[2048,256]{1,0:T(8,128)(2,1)}) %all-gather.9.cloned.1.call-update) | async-done | bytes 1048592 | tf_op jit(solution)/shard_map/all_gather | solution.py:22
  436.7 0.0 copy-start.1
  436.7 0.0 copy-start.7
  436.7 4.6 convolution_multiply_fusion.1
  441.2 0.0 copy-done.1
  441.2 0.0 copy-done.7
  441.2 0.0 copy-start.2
  441.2 2.1 convolution_multiply_fusion.2
  443.3 84.0 %all-gather.11.cloned.1.call-done = bf16[2048,896]{1,0:T(8,128)(2,1)} async-done(((bf16[128,896]{1,0:T(8,128)(2,1)}), bf16[2048,896]{1,0:T(8,128)(2,1)}) %all-gather.11.cloned.1.call-update) | async-done | bytes 3670032 | tf_op jit(solution)/shard_map/all_gather | solution.py:51
  527.3 0.0 copy-done.2
  527.3 4.1 convolution_multiply_fusion
  531.5 78.2 %reduce-scatter.5.cloned.1.call-done = f32[128,256]{1,0:T(8,128)} async-done(((f32[2048,256]{1,0:T(8,128)}), f32[128,256]{1,0:T(8,128)}) %reduce-scatter.5.cloned.1.call-update) | async-done | bytes 131088 | tf_op jit(solution)/shard_map/reduce_scatter | solution.py:53
Async XLA Ops:
  7.2 56.0 %copy-start = (bf16[896,256]{1,0:T(8,128)(2,1)S(1)}, bf16[896,256]{1,0:T(8,128)(2,1)}, u32[]{:S(2)}) copy-start(bf16[896,256]{1,0:T(8,128)(2,1)} %param.13) | copy-start | bytes 1376260
  7.2 56.0 %all-gather.5.cloned.1.call-start = ((), (), s32[]{:S(2)}) async-start(), calls=%async_computation.3 | async-start | bytes 1114112 | tf_op jit(solution)/shard_map/all_gather | solution.py:23
  7.9 221.8 %reduce-scatter.3.cloned.1.call-start = ((), (), s32[]{:S(2)}) async-start(), calls=%async_computation.4 | async-start | bytes 7798784 | tf_op jit(solution)/shard_map/reduce_scatter | solution.py:31
  68.6 161.0 %copy-start.5 = (bf16[128,896]{1,0:T(8,128)(2,1)S(1)}, bf16[128,896]{1,0:T(8,128)(2,1)}, u32[]{:S(2)}) copy-start(bf16[128,896]{1,0:T(8,128)(2,1)} %param.9) | copy-start | bytes 688132
  68.6 161.0 %copy-start.6 = (bf16[128,896]{1,0:T(8,128)(2,1)S(1)}, bf16[128,896]{1,0:T(8,128)(2,1)}, u32[]{:S(2)}) copy-start(bf16[128,896]{1,0:T(8,128)(2,1)} %param.10) | copy-start | bytes 688132
  68.7 315.5 %all-gather.7.cloned.1.call-start = ((), (), s32[]{:S(2)}) async-start(), calls=%async_computation.5 | async-start | bytes 3899392 | tf_op jit(solution)/shard_map/all_gather | solution.py:38
  231.8 204.9 %all-gather.9.cloned.1.call-start = ((), (), s32[]{:S(2)}) async-start(), calls=%async_computation.7 | async-start | bytes 1114112 | tf_op jit(solution)/shard_map/all_gather | solution.py:22
  234.8 149.4 %copy-start.4 = (bf16[896,256]{1,0:T(8,128)(2,1)S(1)}, bf16[896,256]{1,0:T(8,128)(2,1)}, u32[]{:S(2)}) copy-start(bf16[896,256]{1,0:T(8,128)(2,1)} %param.11) | copy-start | bytes 1376260
  234.8 152.7 %all-to-all-start = ((bf16[16,128,896]{2,1,0:T(8,128)(2,1)}), bf16[16,128,896]{2,1,0:T(8,128)(2,1)}, u32[]{:S(2)}, u32[]{:S(2)}) async-start(bf16[16,128,896]{2,1,0:T(8,128)(2,1)} %stack.2), calls=%async_computation.1 | async-start | bytes 7340032 | tf_op jit(solution)/shard_map/all_to_all | solution.py:40
  242.0 285.3 %all-gather.11.cloned.1.call-start = ((), (), s32[]{:S(2)}) async-start(), calls=%async_computation.8 | async-start | bytes 3899392 | tf_op jit(solution)/shard_map/all_gather | solution.py:51
  242.6 144.8 %copy-start.3 = (bf16[896,256]{1,0:T(8,128)(2,1)S(1)}, bf16[896,256]{1,0:T(8,128)(2,1)}, u32[]{:S(2)}) copy-start(bf16[896,256]{1,0:T(8,128)(2,1)} %param.12) | copy-start | bytes 1376260
  242.6 367.0 %reduce-scatter.5.cloned.1.call-start = ((), (), s32[]{:S(2)}) async-start(), calls=%async_computation.6 | async-start | bytes 2228224 | tf_op jit(solution)/shard_map/reduce_scatter | solution.py:53
  436.7 4.6 copy-start.1
  436.7 4.6 copy-start.7
  441.2 86.1 %copy-start.2 = (bf16[2048,256]{1,0:T(8,128)(2,1)S(1)}, bf16[2048,256]{1,0:T(8,128)(2,1)}, u32[]{:S(2)}) copy-start(bf16[2048,256]{1,0:T(8,128)(2,1)} %all-gather.5.cloned.1.call-done) | copy-start | bytes 3145732
Sparse Core Ops, SparseCore 0:
  10.8 52.3 all-gather.4
  68.8 160.8 reduce-scatter.2
  232.0 152.0 all-gather.6
  386.8 49.8 all-gather.8
  438.3 88.9 all-gather.10
  531.9 77.6 reduce-scatter.4
